TPU v7x, 128 devices: a whole 4x4x4 slice. The times are simulated.
128 devices in a mesh: tm: 8 (over x, core), dom: 16 (over z, y).
Axes of the slice: x: 4, y: 4, z: 4, core: 2. Of those that a mesh axis runs over, the one named last changes fastest.
Arguments:
- features: bfloat16 [16, 8192, 128], P('tm', 'dom'), may hold values from -6 to 6
- tile_values: bfloat16 [16, 64, 16, 4, 128, 128], P('tm', 'dom'), may hold values from -0.09375 to 0.09375
- tile_cols: int32 [16, 64, 16, 4], P('tm', 'dom'), may hold values from 0 to 3
- tile_count: int32 [16, 64, 16], P('tm', 'dom'), may hold values from 0 to 4, as said below
- hidden_start: float32 [8192, 512], P('dom'), may hold values from -4 to 4
- w_graph: bfloat16 [128, 512], replicated, may hold values from -0.5 to 0.5
- w_input: bfloat16 [512, 1536], replicated, may hold values from -0.25 to 0.25
- w_hidden: bfloat16 [512, 1536], replicated, may hold values from -0.25 to 0.25
- update_bias: float32 [512], replicated, may hold values from -1 to 4
Outputs:
- hidden_seq: bfloat16 [16, 8192, 512], P('tm', 'dom')
Inputs may be any that keep to these rules, and one draw needn't show every extreme that they name: `tile_count`: number of live slots; for each row block the entry of its own partition is 4.
All inputs are finite; a program needn't handle non-finite values.
Results may differ from a plain program's by a relative error of at most 0.0052.
Values may be sent and summed in bfloat16 or wider, within the bound.
A program may use at most 128 MiB of HBM per device.

v0:
```python
import jax
import jax.numpy as jnp
from jax import lax
from jax.sharding import PartitionSpec as P


def shifted(block, axis, distance):
    devices = range(lax.axis_size(axis))
    route = [((i - distance) % len(devices), i) for i in devices]
    return lax.ppermute(block, axis, route)


def gru_cell(state, gx, w_hidden, update_bias, hid):
    gh = jnp.dot(state.astype(jnp.bfloat16), w_hidden, preferred_element_type=jnp.float32)
    reset = jax.nn.sigmoid(gx[:, :hid] + gh[:, :hid])
    update = jax.nn.sigmoid(gx[:, hid : 2 * hid] + gh[:, hid : 2 * hid] + update_bias)
    cand = jnp.tanh(gx[:, 2 * hid :] + reset * gh[:, 2 * hid :])
    return update * state + (1.0 - update) * cand


def per_device(
    features,
    tile_values,
    tile_cols,
    tile_count,
    hidden_start,
    w_graph,
    w_input,
    w_hidden,
    update_bias,
):
    snaps, nodes, feats = features.shape
    hid = w_graph.shape[1]
    blk = tile_values.shape[-1]
    slot_count = tile_cols.shape[-1]
    nblocks = nodes // blk
    parts = lax.axis_size("dom")
    me_dom = lax.axis_index("dom")
    projected = jnp.einsum(
        "snf,fh->snh", features, w_graph, preferred_element_type=jnp.float32
    ).astype(jnp.bfloat16)
    live = jnp.arange(slot_count, dtype=jnp.int32)[None, None, None, :] < tile_count[..., None]
    masked = tile_values * live[..., None, None].astype(jnp.bfloat16)

    def partner_sum(rows, source):
        tiles_src = lax.dynamic_index_in_dim(masked, source, axis=2, keepdims=False)
        cols_src = lax.dynamic_index_in_dim(tile_cols, source, axis=2, keepdims=False)
        blocks = rows.reshape(snaps, nblocks, blk, hid)
        picked = jax.vmap(lambda block_set, col_set: block_set[col_set])(blocks, cols_src)
        return jnp.einsum(
            "snkij,snkjh->snih", tiles_src, picked, preferred_element_type=jnp.float32
        )

    total = partner_sum(projected, me_dom)

    def loop_step(step, carry):
        rows, acc = carry
        rows = shifted(rows, "dom", 1)
        source = (me_dom - step) % parts
        return (rows, acc + partner_sum(rows, source))

    moved, total = lax.fori_loop(1, parts, loop_step, (projected, total))
    propagated = total.reshape(snaps, nodes, hid)
    graph_out = jax.nn.relu(propagated).astype(jnp.bfloat16)
    sections = lax.axis_size("tm")
    me_time = lax.axis_index("tm")
    mine = lax.all_to_all(graph_out, "tm", split_axis=1, concat_axis=0, tiled=True)
    share = nodes // sections
    start_rows = lax.dynamic_slice_in_dim(hidden_start, me_time * share, share, 0)

    def scan_cell(state, graph_row):
        gx = jnp.dot(graph_row, w_input, preferred_element_type=jnp.float32)
        state = gru_cell(state, gx, w_hidden, update_bias, hid)
        return (state, state.astype(jnp.bfloat16))

    last_state, own_seq = lax.scan(scan_cell, start_rows, mine)
    hidden_seq = lax.all_to_all(own_seq, "tm", split_axis=0, concat_axis=1, tiled=True)
    return hidden_seq


def solution(mesh):
    placed = (
        P("tm", "dom", None),
        P("tm", "dom", None, None, None, None),
        P("tm", "dom", None, None),
        P("tm", "dom", None),
        P("dom", None),
        P(),
        P(),
        P(),
        P(),
    )
    return jax.shard_map(
        per_device, mesh=mesh, in_specs=placed, out_specs=P("tm", "dom", None), check_vma=False
    )
```

profile of v0, /device:TPU:1, one launch (start us, length us, event | category | flops | bytes accessed | tf_op | source)
XLA Modules:
  0.0 593.3 jit_solution(4819321105455400747)
XLA Ops:
  4.3 2.8 gather_fusion.1
  7.1 8.5 %copy_multiply_fusion = bf16[2,4,16,4,128,128]{5,4,3,1,0,2:T(8,128)(2,1)S(1)} fusion(bf16[2,4,16,4,128,128]{5,4,3,2,1,0:T(8,128)(2,1)} %param.14, bf16[2,4,16,4]{3,1,0,2:T(4,128)(2,1)S(1)} %fusion.28), kind=kLoop, calls=%fused_computation.33 | loop fusion | flops 8388608 | bytes 33555456 | tf_op jit(solution)/shard_map/mul | solution.py:43
  15.6 2.5 convolution_bitcast_fusion
  18.1 3.9 copy-done.2
  22.0 450.5 %while.29 = (s32[]{:T(128)}, bf16[2,512,512]{2,1,0:T(8,128)(2,1)S(1)}, f32[2,4,128,512]{3,2,1,0:T(8,128)}, s32[]{:T(128)}, bf16[2,4,16,4,128,128]{5,4,3,1,0,2:T(...) while((s32[]{:T(128)}, ...), condition=%wide.region_1.2_spmd, body=%wide.region_0.1_spmd.sunk | while | flops 537395456 | bytes 24118320 | solution.py:62
  22.0 2.1 collective-permute-start
  24.2 27.7 %collective-permute-done = bf16[2,512,512]{2,1,0:T(8,128)(2,1)S(1)} collective-permute-done((bf16[2,512,512]{2,1,0:T(8,128)(2,1)S(1)}, bf16[2,512,512]{2,1,0:T(8,128)(2,1)S(1)}, u32[]{:S(2)}, u32[]{:S(2)}) %collective-permute-start) | collective-permute-done | bytes 1048608 | tf_op jit(solution)/shard_map/while/body/eval_jaxpr/ppermute | solution.py:10
  51.8 2.8 gather_fusion
  54.6 5.2 bitcast_add_fusion.2
  60.1 26.6 %collective-permute-done = bf16[2,512,512]{2,1,0:T(8,128)(2,1)S(1)} collective-permute-done((bf16[2,512,512]{2,1,0:T(8,128)(2,1)S(1)}, bf16[2,512,512]{2,1,0:T(8,128)(2,1)S(1)}, u32[]{:S(2)}, u32[]{:S(2)}) %collective-permute-start) | collective-permute-done | bytes 1048608 | tf_op jit(solution)/shard_map/while/body/eval_jaxpr/ppermute | solution.py:10
  86.8 2.8 gather_fusion
  89.5 5.2 bitcast_add_fusion.2
  95.0 25.8 %collective-permute-done = bf16[2,512,512]{2,1,0:T(8,128)(2,1)S(1)} collective-permute-done((bf16[2,512,512]{2,1,0:T(8,128)(2,1)S(1)}, bf16[2,512,512]{2,1,0:T(8,128)(2,1)S(1)}, u32[]{:S(2)}, u32[]{:S(2)}) %collective-permute-start) | collective-permute-done | bytes 1048608 | tf_op jit(solution)/shard_map/while/body/eval_jaxpr/ppermute | solution.py:10
  120.8 2.8 gather_fusion
  123.5 5.2 bitcast_add_fusion.2
  129.1 24.9 %collective-permute-done = bf16[2,512,512]{2,1,0:T(8,128)(2,1)S(1)} collective-permute-done((bf16[2,512,512]{2,1,0:T(8,128)(2,1)S(1)}, bf16[2,512,512]{2,1,0:T(8,128)(2,1)S(1)}, u32[]{:S(2)}, u32[]{:S(2)}) %collective-permute-start) | collective-permute-done | bytes 1048608 | tf_op jit(solution)/shard_map/while/body/eval_jaxpr/ppermute | solution.py:10
  154.0 2.8 gather_fusion
  156.7 5.2 bitcast_add_fusion.2
  162.2 24.1 %collective-permute-done = bf16[2,512,512]{2,1,0:T(8,128)(2,1)S(1)} collective-permute-done((bf16[2,512,512]{2,1,0:T(8,128)(2,1)S(1)}, bf16[2,512,512]{2,1,0:T(8,128)(2,1)S(1)}, u32[]{:S(2)}, u32[]{:S(2)}) %collective-permute-start) | collective-permute-done | bytes 1048608 | tf_op jit(solution)/shard_map/while/body/eval_jaxpr/ppermute | solution.py:10
  186.3 2.8 gather_fusion
  189.1 5.2 bitcast_add_fusion.2
  194.6 23.2 %collective-permute-done = bf16[2,512,512]{2,1,0:T(8,128)(2,1)S(1)} collective-permute-done((bf16[2,512,512]{2,1,0:T(8,128)(2,1)S(1)}, bf16[2,512,512]{2,1,0:T(8,128)(2,1)S(1)}, u32[]{:S(2)}, u32[]{:S(2)}) %collective-permute-start) | collective-permute-done | bytes 1048608 | tf_op jit(solution)/shard_map/while/body/eval_jaxpr/ppermute | solution.py:10
  217.8 2.8 gather_fusion
  220.5 5.2 bitcast_add_fusion.2
  226.1 22.4 %collective-permute-done = bf16[2,512,512]{2,1,0:T(8,128)(2,1)S(1)} collective-permute-done((bf16[2,512,512]{2,1,0:T(8,128)(2,1)S(1)}, bf16[2,512,512]{2,1,0:T(8,128)(2,1)S(1)}, u32[]{:S(2)}, u32[]{:S(2)}) %collective-permute-start) | collective-permute-done | bytes 1048608 | tf_op jit(solution)/shard_map/while/body/eval_jaxpr/ppermute | solution.py:10
  248.4 2.8 gather_fusion
  251.2 5.2 bitcast_add_fusion.2
  256.7 21.5 %collective-permute-done = bf16[2,512,512]{2,1,0:T(8,128)(2,1)S(1)} collective-permute-done((bf16[2,512,512]{2,1,0:T(8,128)(2,1)S(1)}, bf16[2,512,512]{2,1,0:T(8,128)(2,1)S(1)}, u32[]{:S(2)}, u32[]{:S(2)}) %collective-permute-start) | collective-permute-done | bytes 1048608 | tf_op jit(solution)/shard_map/while/body/eval_jaxpr/ppermute | solution.py:10
  278.2 2.8 gather_fusion
  280.9 5.2 bitcast_add_fusion.2
  286.4 20.6 %collective-permute-done = bf16[2,512,512]{2,1,0:T(8,128)(2,1)S(1)} collective-permute-done((bf16[2,512,512]{2,1,0:T(8,128)(2,1)S(1)}, bf16[2,512,512]{2,1,0:T(8,128)(2,1)S(1)}, u32[]{:S(2)}, u32[]{:S(2)}) %collective-permute-start) | collective-permute-done | bytes 1048608 | tf_op jit(solution)/shard_map/while/body/eval_jaxpr/ppermute | solution.py:10
  307.1 2.8 gather_fusion
  309.8 5.2 bitcast_add_fusion.2
  315.4 19.8 %collective-permute-done = bf16[2,512,512]{2,1,0:T(8,128)(2,1)S(1)} collective-permute-done((bf16[2,512,512]{2,1,0:T(8,128)(2,1)S(1)}, bf16[2,512,512]{2,1,0:T(8,128)(2,1)S(1)}, u32[]{:S(2)}, u32[]{:S(2)}) %collective-permute-start) | collective-permute-done | bytes 1048608 | tf_op jit(solution)/shard_map/while/body/eval_jaxpr/ppermute | solution.py:10
  335.1 2.8 gather_fusion
  337.9 5.2 bitcast_add_fusion.2
  343.4 18.9 %collective-permute-done = bf16[2,512,512]{2,1,0:T(8,128)(2,1)S(1)} collective-permute-done((bf16[2,512,512]{2,1,0:T(8,128)(2,1)S(1)}, bf16[2,512,512]{2,1,0:T(8,128)(2,1)S(1)}, u32[]{:S(2)}, u32[]{:S(2)}) %collective-permute-start) | collective-permute-done | bytes 1048608 | tf_op jit(solution)/shard_map/while/body/eval_jaxpr/ppermute | solution.py:10
  362.3 2.8 gather_fusion
  365.1 5.2 bitcast_add_fusion.2
  370.6 18.1 %collective-permute-done = bf16[2,512,512]{2,1,0:T(8,128)(2,1)S(1)} collective-permute-done((bf16[2,512,512]{2,1,0:T(8,128)(2,1)S(1)}, bf16[2,512,512]{2,1,0:T(8,128)(2,1)S(1)}, u32[]{:S(2)}, u32[]{:S(2)}) %collective-permute-start) | collective-permute-done | bytes 1048608 | tf_op jit(solution)/shard_map/while/body/eval_jaxpr/ppermute | solution.py:10
  388.7 2.8 gather_fusion
  391.4 5.2 bitcast_add_fusion.2
  397.0 17.2 %collective-permute-done = bf16[2,512,512]{2,1,0:T(8,128)(2,1)S(1)} collective-permute-done((bf16[2,512,512]{2,1,0:T(8,128)(2,1)S(1)}, bf16[2,512,512]{2,1,0:T(8,128)(2,1)S(1)}, u32[]{:S(2)}, u32[]{:S(2)}) %collective-permute-start) | collective-permute-done | bytes 1048608 | tf_op jit(solution)/shard_map/while/body/eval_jaxpr/ppermute | solution.py:10
  414.2 2.8 gather_fusion
  416.9 5.2 bitcast_add_fusion.2
  422.4 16.8 %collective-permute-done = bf16[2,512,512]{2,1,0:T(8,128)(2,1)S(1)} collective-permute-done((bf16[2,512,512]{2,1,0:T(8,128)(2,1)S(1)}, bf16[2,512,512]{2,1,0:T(8,128)(2,1)S(1)}, u32[]{:S(2)}, u32[]{:S(2)}) %collective-permute-start) | collective-permute-done | bytes 1048608 | tf_op jit(solution)/shard_map/while/body/eval_jaxpr/ppermute | solution.py:10
  439.3 2.8 gather_fusion
  442.0 5.2 bitcast_add_fusion.2
  447.5 16.8 %collective-permute-done = bf16[2,512,512]{2,1,0:T(8,128)(2,1)S(1)} collective-permute-done((bf16[2,512,512]{2,1,0:T(8,128)(2,1)S(1)}, bf16[2,512,512]{2,1,0:T(8,128)(2,1)S(1)}, u32[]{:S(2)}, u32[]{:S(2)}) %collective-permute-start) | collective-permute-done | bytes 1048608 | tf_op jit(solution)/shard_map/while/body/eval_jaxpr/ppermute | solution.py:10
  464.4 2.8 gather_fusion
  467.1 5.2 bitcast_add_fusion.2
  472.4 1.9 maximum_convert_fusion
  474.3 2.1 copy.26
  476.4 18.2 %all-to-all-start = ((bf16[2,512,512]{2,0,1:T(2,128)(2,1)}), bf16[2,512,512]{2,0,1:T(2,128)(2,1)}, u32[]{:S(2)}, u32[]{:S(2)}) async-start(bf16[2,512,512]{2,0,1:T(2,128)(2,1)} %bitcast.70), calls=%async_computation | async-start | bytes 2097152 | tf_op jit(solution)/shard_map/all_to_all | solution.py:67
  494.6 15.1 %all-to-all-done = bf16[2,512,512]{2,0,1:T(2,128)(2,1)} async-done(((bf16[2,512,512]{2,0,1:T(2,128)(2,1)}), bf16[2,512,512]{2,0,1:T(2,128)(2,1)}, u32[]{:S(2)}, u32[]{:S(2)}) %all-to-all-start) | async-done | bytes 1048608 | tf_op jit(solution)/shard_map/all_to_all | solution.py:67
  512.2 60.7 %while.30 = (s32[]{:T(128)}, f32[64,512]{1,0:T(8,128)S(1)}, bf16[16,64,512]{2,1,0:T(8,128)(2,1)}, bf16[16,64,512]{2,1,0:T(8,128)(2,1)}, bf16[512,1536]{1,0:T(8,1...) while((s32[]{:T(128)}, f32[64,512]{1,0:T(8,128)S(1)}, ...), condition=%wide.region_3.4_spmd, body=%wide.region_2.3_spmd.sunk | while | flops 201883648 | bytes 5246037 | solution.py:76
  517.2 1.8 fusion.55
  521.0 1.8 fusion.55
  528.6 1.8 fusion.55
  532.3 1.8 fusion.55
  536.1 1.8 fusion.55
  543.7 1.8 fusion.55
  562.7 1.8 fusion.55
  572.8 19.4 %all_to_all.36 = bf16[16,64,512]{2,1,0:T(8,128)(2,1)S(1)} all-to-all(bf16[16,64,512]{2,1,0:T(8,128)(2,1)} %get-tuple-element.198), channel_id=1, replica_groups=mesh['tm'=8,'dom'=16] {'tm'}, dimensions={0} | all-to-all | bytes 2097152 | tf_op jit(solution)/shard_map/all_to_all | solution.py:77
  (121 shorter events, 59.4 us)
Async XLA Ops:
  0.0 494.6 %copy-start = (f32[512,512]{1,0:T(8,128)S(1)}, f32[512,512]{1,0:T(8,128)}, u32[]{:S(2)}) copy-start(f32[512,512]{1,0:T(8,128)} %param.17) | copy-start | bytes 3145732
  7.1 8.5 %copy-start.3 = (bf16[32,128,512]{2,1,0:T(8,128)(2,1)S(1)}, bf16[32,128,512]{2,1,0:T(8,128)(2,1)}, u32[]{:S(2)}) copy-start(bf16[32,128,512]{2,1,0:T(8,128)(2,1)} %gather_fusion.1) | copy-start | bytes 12582916
  15.6 6.4 %copy-start.2 = (bf16[2,4,16,4,128,128]{5,4,3,1,0,2:T(8,128)(2,1)}, bf16[2,4,16,4,128,128]{5,4,3,1,0,2:T(8,128)(2,1)S(1)}, u32[]{:S(2)}) copy-start(bf16[2,4,16,4,128,128]{5,4,3,1,0,2:T(8,128)(2,1)S(1)} %copy_multiply_fusion) | copy-start | bytes 50331652
  22.0 29.9 %collective-permute-start = (bf16[2,512,512]{2,1,0:T(8,128)(2,1)S(1)}, bf16[2,512,512]{2,1,0:T(8,128)(2,1)S(1)}, u32[]{:S(2)}, u32[]{:S(2)}) collective-permute-start(bf16[2,512,512]{2,1,0:T(8,128)(2,1)S(1)} %get-tuple-element.346), channel_id=1, source_target_pairs={{15,0},{0,1},{1,2},{2,3},{3,4},{4,5},{5,6},{6,7},{7,8},{8,9},{9,10... | collective-permute-start | bytes 3145736 | tf_op jit(solution)/shard_map/while/body/eval_jaxpr/ppermute | solution.py:10
  59.9 26.9 %collective-permute-start = (bf16[2,512,512]{2,1,0:T(8,128)(2,1)S(1)}, bf16[2,512,512]{2,1,0:T(8,128)(2,1)S(1)}, u32[]{:S(2)}, u32[]{:S(2)}) collective-permute-start(bf16[2,512,512]{2,1,0:T(8,128)(2,1)S(1)} %get-tuple-element.346), channel_id=1, source_target_pairs={{15,0},{0,1},{1,2},{2,3},{3,4},{4,5},{5,6},{6,7},{7,8},{8,9},{9,10... | collective-permute-start | bytes 3145736 | tf_op jit(solution)/shard_map/while/body/eval_jaxpr/ppermute | solution.py:10
  94.8 26.0 %collective-permute-start = (bf16[2,512,512]{2,1,0:T(8,128)(2,1)S(1)}, bf16[2,512,512]{2,1,0:T(8,128)(2,1)S(1)}, u32[]{:S(2)}, u32[]{:S(2)}) collective-permute-start(bf16[2,512,512]{2,1,0:T(8,128)(2,1)S(1)} %get-tuple-element.346), channel_id=1, source_target_pairs={{15,0},{0,1},{1,2},{2,3},{3,4},{4,5},{5,6},{6,7},{7,8},{8,9},{9,10... | collective-permute-start | bytes 3145736 | tf_op jit(solution)/shard_map/while/body/eval_jaxpr/ppermute | solution.py:10
  128.9 25.1 %collective-permute-start = (bf16[2,512,512]{2,1,0:T(8,128)(2,1)S(1)}, bf16[2,512,512]{2,1,0:T(8,128)(2,1)S(1)}, u32[]{:S(2)}, u32[]{:S(2)}) collective-permute-start(bf16[2,512,512]{2,1,0:T(8,128)(2,1)S(1)} %get-tuple-element.346), channel_id=1, source_target_pairs={{15,0},{0,1},{1,2},{2,3},{3,4},{4,5},{5,6},{6,7},{7,8},{8,9},{9,10... | collective-permute-start | bytes 3145736 | tf_op jit(solution)/shard_map/while/body/eval_jaxpr/ppermute | solution.py:10
  162.0 24.3 %collective-permute-start = (bf16[2,512,512]{2,1,0:T(8,128)(2,1)S(1)}, bf16[2,512,512]{2,1,0:T(8,128)(2,1)S(1)}, u32[]{:S(2)}, u32[]{:S(2)}) collective-permute-start(bf16[2,512,512]{2,1,0:T(8,128)(2,1)S(1)} %get-tuple-element.346), channel_id=1, source_target_pairs={{15,0},{0,1},{1,2},{2,3},{3,4},{4,5},{5,6},{6,7},{7,8},{8,9},{9,10... | collective-permute-start | bytes 3145736 | tf_op jit(solution)/shard_map/while/body/eval_jaxpr/ppermute | solution.py:10
  194.4 23.4 %collective-permute-start = (bf16[2,512,512]{2,1,0:T(8,128)(2,1)S(1)}, bf16[2,512,512]{2,1,0:T(8,128)(2,1)S(1)}, u32[]{:S(2)}, u32[]{:S(2)}) collective-permute-start(bf16[2,512,512]{2,1,0:T(8,128)(2,1)S(1)} %get-tuple-element.346), channel_id=1, source_target_pairs={{15,0},{0,1},{1,2},{2,3},{3,4},{4,5},{5,6},{6,7},{7,8},{8,9},{9,10... | collective-permute-start | bytes 3145736 | tf_op jit(solution)/shard_map/while/body/eval_jaxpr/ppermute | solution.py:10
  225.8 22.6 %collective-permute-start = (bf16[2,512,512]{2,1,0:T(8,128)(2,1)S(1)}, bf16[2,512,512]{2,1,0:T(8,128)(2,1)S(1)}, u32[]{:S(2)}, u32[]{:S(2)}) collective-permute-start(bf16[2,512,512]{2,1,0:T(8,128)(2,1)S(1)} %get-tuple-element.346), channel_id=1, source_target_pairs={{15,0},{0,1},{1,2},{2,3},{3,4},{4,5},{5,6},{6,7},{7,8},{8,9},{9,10... | collective-permute-start | bytes 3145736 | tf_op jit(solution)/shard_map/while/body/eval_jaxpr/ppermute | solution.py:10
  256.5 21.7 %collective-permute-start = (bf16[2,512,512]{2,1,0:T(8,128)(2,1)S(1)}, bf16[2,512,512]{2,1,0:T(8,128)(2,1)S(1)}, u32[]{:S(2)}, u32[]{:S(2)}) collective-permute-start(bf16[2,512,512]{2,1,0:T(8,128)(2,1)S(1)} %get-tuple-element.346), channel_id=1, source_target_pairs={{15,0},{0,1},{1,2},{2,3},{3,4},{4,5},{5,6},{6,7},{7,8},{8,9},{9,10... | collective-permute-start | bytes 3145736 | tf_op jit(solution)/shard_map/while/body/eval_jaxpr/ppermute | solution.py:10
  286.2 20.8 %collective-permute-start = (bf16[2,512,512]{2,1,0:T(8,128)(2,1)S(1)}, bf16[2,512,512]{2,1,0:T(8,128)(2,1)S(1)}, u32[]{:S(2)}, u32[]{:S(2)}) collective-permute-start(bf16[2,512,512]{2,1,0:T(8,128)(2,1)S(1)} %get-tuple-element.346), channel_id=1, source_target_pairs={{15,0},{0,1},{1,2},{2,3},{3,4},{4,5},{5,6},{6,7},{7,8},{8,9},{9,10... | collective-permute-start | bytes 3145736 | tf_op jit(solution)/shard_map/while/body/eval_jaxpr/ppermute | solution.py:10
  315.1 20.0 %collective-permute-start = (bf16[2,512,512]{2,1,0:T(8,128)(2,1)S(1)}, bf16[2,512,512]{2,1,0:T(8,128)(2,1)S(1)}, u32[]{:S(2)}, u32[]{:S(2)}) collective-permute-start(bf16[2,512,512]{2,1,0:T(8,128)(2,1)S(1)} %get-tuple-element.346), channel_id=1, source_target_pairs={{15,0},{0,1},{1,2},{2,3},{3,4},{4,5},{5,6},{6,7},{7,8},{8,9},{9,10... | collective-permute-start | bytes 3145736 | tf_op jit(solution)/shard_map/while/body/eval_jaxpr/ppermute | solution.py:10
  343.2 19.1 %collective-permute-start = (bf16[2,512,512]{2,1,0:T(8,128)(2,1)S(1)}, bf16[2,512,512]{2,1,0:T(8,128)(2,1)S(1)}, u32[]{:S(2)}, u32[]{:S(2)}) collective-permute-start(bf16[2,512,512]{2,1,0:T(8,128)(2,1)S(1)} %get-tuple-element.346), channel_id=1, source_target_pairs={{15,0},{0,1},{1,2},{2,3},{3,4},{4,5},{5,6},{6,7},{7,8},{8,9},{9,10... | collective-permute-start | bytes 3145736 | tf_op jit(solution)/shard_map/while/body/eval_jaxpr/ppermute | solution.py:10
  370.4 18.3 %collective-permute-start = (bf16[2,512,512]{2,1,0:T(8,128)(2,1)S(1)}, bf16[2,512,512]{2,1,0:T(8,128)(2,1)S(1)}, u32[]{:S(2)}, u32[]{:S(2)}) collective-permute-start(bf16[2,512,512]{2,1,0:T(8,128)(2,1)S(1)} %get-tuple-element.346), channel_id=1, source_target_pairs={{15,0},{0,1},{1,2},{2,3},{3,4},{4,5},{5,6},{6,7},{7,8},{8,9},{9,10... | collective-permute-start | bytes 3145736 | tf_op jit(solution)/shard_map/while/body/eval_jaxpr/ppermute | solution.py:10
  396.7 17.4 %collective-permute-start = (bf16[2,512,512]{2,1,0:T(8,128)(2,1)S(1)}, bf16[2,512,512]{2,1,0:T(8,128)(2,1)S(1)}, u32[]{:S(2)}, u32[]{:S(2)}) collective-permute-start(bf16[2,512,512]{2,1,0:T(8,128)(2,1)S(1)} %get-tuple-element.346), channel_id=1, source_target_pairs={{15,0},{0,1},{1,2},{2,3},{3,4},{4,5},{5,6},{6,7},{7,8},{8,9},{9,10... | collective-permute-start | bytes 3145736 | tf_op jit(solution)/shard_map/while/body/eval_jaxpr/ppermute | solution.py:10
  422.2 17.0 %collective-permute-start = (bf16[2,512,512]{2,1,0:T(8,128)(2,1)S(1)}, bf16[2,512,512]{2,1,0:T(8,128)(2,1)S(1)}, u32[]{:S(2)}, u32[]{:S(2)}) collective-permute-start(bf16[2,512,512]{2,1,0:T(8,128)(2,1)S(1)} %get-tuple-element.346), channel_id=1, source_target_pairs={{15,0},{0,1},{1,2},{2,3},{3,4},{4,5},{5,6},{6,7},{7,8},{8,9},{9,10... | collective-permute-start | bytes 3145736 | tf_op jit(solution)/shard_map/while/body/eval_jaxpr/ppermute | solution.py:10
  447.3 17.0 %collective-permute-start = (bf16[2,512,512]{2,1,0:T(8,128)(2,1)S(1)}, bf16[2,512,512]{2,1,0:T(8,128)(2,1)S(1)}, u32[]{:S(2)}, u32[]{:S(2)}) collective-permute-start(bf16[2,512,512]{2,1,0:T(8,128)(2,1)S(1)} %get-tuple-element.346), channel_id=1, source_target_pairs={{15,0},{0,1},{1,2},{2,3},{3,4},{4,5},{5,6},{6,7},{7,8},{8,9},{9,10... | collective-permute-start | bytes 3145736 | tf_op jit(solution)/shard_map/while/body/eval_jaxpr/ppermute | solution.py:10
  474.3 37.9 %copy-start.1 = (bf16[512,1536]{1,0:T(8,128)(2,1)S(1)}, bf16[512,1536]{1,0:T(8,128)(2,1)}, u32[]{:S(2)}) copy-start(bf16[512,1536]{1,0:T(8,128)(2,1)} %param.19) | copy-start | bytes 4718596
  474.3 37.9 %copy-start.4 = (f32[512]{0:T(512)S(1)}, f32[512]{0:T(512)}, u32[]{:S(2)}) copy-start(f32[512]{0:T(512)} %param.21) | copy-start | bytes 6148
  476.4 33.3 %all-to-all-start = ((bf16[2,512,512]{2,0,1:T(2,128)(2,1)}), bf16[2,512,512]{2,0,1:T(2,128)(2,1)}, u32[]{:S(2)}, u32[]{:S(2)}) async-start(bf16[2,512,512]{2,0,1:T(2,128)(2,1)} %bitcast.70), calls=%async_computation | async-start | bytes 2097152 | tf_op jit(solution)/shard_map/all_to_all | solution.py:67
where the time goes:
time: 595 us; the launch traced here: 593 us
  waiting for transfers between devices  339 us (57%)
  matrix products  130 us (22%)
  local copies, waits for them, and re-layouts  58.6 us (10%)
  other arithmetic  23 us (4%)
  starting transfers between devices  21.4 us (4%)
  blocking collectives  19.4 us (3%)
    ppermute x15, waiting for transfers between devices, shifted(): return lax.ppermute(block, axis, route)  324 us
    dot_general x16, matrix products, partner_sum(): jnp.einsum('snkij,snkjh->snih', tiles_src, picked, preferred_element_type...  80.8 us
    gather x32, local copies, waits for them, and re-layouts, partner_sum(): block_set[col_set]  45.4 us
    dot_general x16, matrix products, gru_cell(): jnp.dot(state.astype(jnp.bfloat16), w_hidden, preferred_element_type=jnp....  28.7 us
    dot_general x16, matrix products, scan_cell(): gx = jnp.dot(graph_row, w_input, preferred_element_type=jnp.float32)  19.5 us
    all_to_all x1, blocking collectives, per_device(): lax.all_to_all(own_seq, 'tm', split_axis=0, concat_axis=1, tiled=True)  19.4 us
    all_to_all x1, starting transfers between devices, per_device(): lax.all_to_all(graph_out, 'tm', split_axis=1, concat_axis=0, tiled=True)  18.2 us
    all_to_all x1, waiting for transfers between devices, per_device(): lax.all_to_all(graph_out, 'tm', split_axis=1, concat_axis=0, tiled=True)  15.1 us
  transfers between devices with their start and end apart: 16, of which 16 were waited for; matrix products, arithmetic and copies ran while one was open for 0% of the time, Pallas kernels for 0%

commit v1 on v0

--- a/solution.py
+++ b/solution.py
@@ -64,7 +64,10 @@
     graph_out = jax.nn.relu(propagated).astype(jnp.bfloat16)
     sections = lax.axis_size("tm")
     me_time = lax.axis_index("tm")
-    mine = lax.all_to_all(graph_out, "tm", split_axis=1, concat_axis=0, tiled=True)
+    mine = jnp.concatenate(
+        lax.all_to_all(jnp.stack(jnp.split(graph_out, lax.axis_size("tm"), axis=1)), "tm", 0, 0),
+        axis=0,
+    )
     share = nodes // sections
     start_rows = lax.dynamic_slice_in_dim(hidden_start, me_time * share, share, 0)
 

time: 595 us -> 596 us (level)
  no operation moved by 1% of the time
where the time goes in v1:
time: 596 us; the launch traced here: 594 us
  waiting for transfers between devices  339 us (57%)
  matrix products  130 us (22%)
  local copies, waits for them, and re-layouts  59.4 us (10%)
  other arithmetic  23.1 us (4%)
  starting transfers between devices  21.4 us (4%)
  blocking collectives  19.4 us (3%)
    ppermute x15, waiting for transfers between devices, shifted(): return lax.ppermute(block, axis, route)  324 us
    dot_general x16, matrix products, partner_sum(): jnp.einsum('snkij,snkjh->snih', tiles_src, picked, preferred_element_type...  80.8 us
    gather x32, local copies, waits for them, and re-layouts, partner_sum(): block_set[col_set]  45.4 us
    dot_general x16, matrix products, gru_cell(): jnp.dot(state.astype(jnp.bfloat16), w_hidden, preferred_element_type=jnp....  28.7 us
    dot_general x16, matrix products, scan_cell(): gx = jnp.dot(graph_row, w_input, preferred_element_type=jnp.float32)  19.5 us
    all_to_all x1, blocking collectives, per_device(): lax.all_to_all(own_seq, 'tm', split_axis=0, concat_axis=1, tiled=True)  19.4 us
    all_to_all x1, starting transfers between devices, per_device(): lax.all_to_all(jnp.stack(jnp.split(graph_out, lax.axis_size('tm'), axis=1...  18.2 us
    all_to_all x1, waiting for transfers between devices, per_device(): lax.all_to_all(jnp.stack(jnp.split(graph_out, lax.axis_size('tm'), axis=1...  15.1 us
  transfers between devices with their start and end apart: 16, of which 16 were waited for; matrix products, arithmetic and copies ran while one was open for 0% of the time, Pallas kernels for 0%

profile of v1, /device:TPU:1, one launch (start us, length us, event | category | flops | bytes accessed | tf_op | source)
XLA Modules:
  0.0 594.1 jit_solution(3788291664134091521)
XLA Ops:
  4.3 2.8 gather_fusion.1
  7.1 8.5 %copy_multiply_fusion = bf16[2,4,16,4,128,128]{5,4,3,1,0,2:T(8,128)(2,1)S(1)} fusion(bf16[2,4,16,4,128,128]{5,4,3,2,1,0:T(8,128)(2,1)} %param.14, bf16[2,4,16,4]{3,1,0,2:T(4,128)(2,1)S(1)} %fusion.36), kind=kLoop, calls=%fused_computation.33 | loop fusion | flops 8388608 | bytes 33555456 | tf_op jit(solution)/shard_map/mul | solution.py:43
  15.6 2.5 convolution_bitcast_fusion
  18.1 3.9 copy-done.2
  22.0 450.5 %while.29 = (s32[]{:T(128)}, bf16[2,512,512]{2,1,0:T(8,128)(2,1)S(1)}, f32[2,4,128,512]{3,2,1,0:T(8,128)}, s32[]{:T(128)}, bf16[2,4,16,4,128,128]{5,4,3,1,0,2:T(...) while((s32[]{:T(128)}, ...), condition=%wide.region_1.2_spmd, body=%wide.region_0.1_spmd.sunk | while | flops 537395456 | bytes 24118320 | solution.py:62
  22.0 2.1 collective-permute-start
  24.2 27.7 %collective-permute-done = bf16[2,512,512]{2,1,0:T(8,128)(2,1)S(1)} collective-permute-done((bf16[2,512,512]{2,1,0:T(8,128)(2,1)S(1)}, bf16[2,512,512]{2,1,0:T(8,128)(2,1)S(1)}, u32[]{:S(2)}, u32[]{:S(2)}) %collective-permute-start) | collective-permute-done | bytes 1048608 | tf_op jit(solution)/shard_map/while/body/eval_jaxpr/ppermute | solution.py:10
  51.8 2.8 gather_fusion
  54.6 5.2 bitcast_add_fusion.2
  60.1 26.6 %collective-permute-done = bf16[2,512,512]{2,1,0:T(8,128)(2,1)S(1)} collective-permute-done((bf16[2,512,512]{2,1,0:T(8,128)(2,1)S(1)}, bf16[2,512,512]{2,1,0:T(8,128)(2,1)S(1)}, u32[]{:S(2)}, u32[]{:S(2)}) %collective-permute-start) | collective-permute-done | bytes 1048608 | tf_op jit(solution)/shard_map/while/body/eval_jaxpr/ppermute | solution.py:10
  86.8 2.8 gather_fusion
  89.5 5.2 bitcast_add_fusion.2
  95.0 25.8 %collective-permute-done = bf16[2,512,512]{2,1,0:T(8,128)(2,1)S(1)} collective-permute-done((bf16[2,512,512]{2,1,0:T(8,128)(2,1)S(1)}, bf16[2,512,512]{2,1,0:T(8,128)(2,1)S(1)}, u32[]{:S(2)}, u32[]{:S(2)}) %collective-permute-start) | collective-permute-done | bytes 1048608 | tf_op jit(solution)/shard_map/while/body/eval_jaxpr/ppermute | solution.py:10
  120.8 2.8 gather_fusion
  123.5 5.2 bitcast_add_fusion.2
  129.1 24.9 %collective-permute-done = bf16[2,512,512]{2,1,0:T(8,128)(2,1)S(1)} collective-permute-done((bf16[2,512,512]{2,1,0:T(8,128)(2,1)S(1)}, bf16[2,512,512]{2,1,0:T(8,128)(2,1)S(1)}, u32[]{:S(2)}, u32[]{:S(2)}) %collective-permute-start) | collective-permute-done | bytes 1048608 | tf_op jit(solution)/shard_map/while/body/eval_jaxpr/ppermute | solution.py:10
  154.0 2.8 gather_fusion
  156.7 5.2 bitcast_add_fusion.2
  162.2 24.1 %collective-permute-done = bf16[2,512,512]{2,1,0:T(8,128)(2,1)S(1)} collective-permute-done((bf16[2,512,512]{2,1,0:T(8,128)(2,1)S(1)}, bf16[2,512,512]{2,1,0:T(8,128)(2,1)S(1)}, u32[]{:S(2)}, u32[]{:S(2)}) %collective-permute-start) | collective-permute-done | bytes 1048608 | tf_op jit(solution)/shard_map/while/body/eval_jaxpr/ppermute | solution.py:10
  186.3 2.8 gather_fusion
  189.1 5.2 bitcast_add_fusion.2
  194.6 23.2 %collective-permute-done = bf16[2,512,512]{2,1,0:T(8,128)(2,1)S(1)} collective-permute-done((bf16[2,512,512]{2,1,0:T(8,128)(2,1)S(1)}, bf16[2,512,512]{2,1,0:T(8,128)(2,1)S(1)}, u32[]{:S(2)}, u32[]{:S(2)}) %collective-permute-start) | collective-permute-done | bytes 1048608 | tf_op jit(solution)/shard_map/while/body/eval_jaxpr/ppermute | solution.py:10
  217.8 2.8 gather_fusion
  220.5 5.2 bitcast_add_fusion.2
  226.1 22.4 %collective-permute-done = bf16[2,512,512]{2,1,0:T(8,128)(2,1)S(1)} collective-permute-done((bf16[2,512,512]{2,1,0:T(8,128)(2,1)S(1)}, bf16[2,512,512]{2,1,0:T(8,128)(2,1)S(1)}, u32[]{:S(2)}, u32[]{:S(2)}) %collective-permute-start) | collective-permute-done | bytes 1048608 | tf_op jit(solution)/shard_map/while/body/eval_jaxpr/ppermute | solution.py:10
  248.4 2.8 gather_fusion
  251.2 5.2 bitcast_add_fusion.2
  256.7 21.5 %collective-permute-done = bf16[2,512,512]{2,1,0:T(8,128)(2,1)S(1)} collective-permute-done((bf16[2,512,512]{2,1,0:T(8,128)(2,1)S(1)}, bf16[2,512,512]{2,1,0:T(8,128)(2,1)S(1)}, u32[]{:S(2)}, u32[]{:S(2)}) %collective-permute-start) | collective-permute-done | bytes 1048608 | tf_op jit(solution)/shard_map/while/body/eval_jaxpr/ppermute | solution.py:10
  278.2 2.8 gather_fusion
  280.9 5.2 bitcast_add_fusion.2
  286.4 20.6 %collective-permute-done = bf16[2,512,512]{2,1,0:T(8,128)(2,1)S(1)} collective-permute-done((bf16[2,512,512]{2,1,0:T(8,128)(2,1)S(1)}, bf16[2,512,512]{2,1,0:T(8,128)(2,1)S(1)}, u32[]{:S(2)}, u32[]{:S(2)}) %collective-permute-start) | collective-permute-done | bytes 1048608 | tf_op jit(solution)/shard_map/while/body/eval_jaxpr/ppermute | solution.py:10
  307.1 2.8 gather_fusion
  309.8 5.2 bitcast_add_fusion.2
  315.4 19.8 %collective-permute-done = bf16[2,512,512]{2,1,0:T(8,128)(2,1)S(1)} collective-permute-done((bf16[2,512,512]{2,1,0:T(8,128)(2,1)S(1)}, bf16[2,512,512]{2,1,0:T(8,128)(2,1)S(1)}, u32[]{:S(2)}, u32[]{:S(2)}) %collective-permute-start) | collective-permute-done | bytes 1048608 | tf_op jit(solution)/shard_map/while/body/eval_jaxpr/ppermute | solution.py:10
  335.1 2.8 gather_fusion
  337.9 5.2 bitcast_add_fusion.2
  343.4 18.9 %collective-permute-done = bf16[2,512,512]{2,1,0:T(8,128)(2,1)S(1)} collective-permute-done((bf16[2,512,512]{2,1,0:T(8,128)(2,1)S(1)}, bf16[2,512,512]{2,1,0:T(8,128)(2,1)S(1)}, u32[]{:S(2)}, u32[]{:S(2)}) %collective-permute-start) | collective-permute-done | bytes 1048608 | tf_op jit(solution)/shard_map/while/body/eval_jaxpr/ppermute | solution.py:10
  362.3 2.8 gather_fusion
  365.1 5.2 bitcast_add_fusion.2
  370.6 18.1 %collective-permute-done = bf16[2,512,512]{2,1,0:T(8,128)(2,1)S(1)} collective-permute-done((bf16[2,512,512]{2,1,0:T(8,128)(2,1)S(1)}, bf16[2,512,512]{2,1,0:T(8,128)(2,1)S(1)}, u32[]{:S(2)}, u32[]{:S(2)}) %collective-permute-start) | collective-permute-done | bytes 1048608 | tf_op jit(solution)/shard_map/while/body/eval_jaxpr/ppermute | solution.py:10
  388.7 2.8 gather_fusion
  391.4 5.2 bitcast_add_fusion.2
  397.0 17.2 %collective-permute-done = bf16[2,512,512]{2,1,0:T(8,128)(2,1)S(1)} collective-permute-done((bf16[2,512,512]{2,1,0:T(8,128)(2,1)S(1)}, bf16[2,512,512]{2,1,0:T(8,128)(2,1)S(1)}, u32[]{:S(2)}, u32[]{:S(2)}) %collective-permute-start) | collective-permute-done | bytes 1048608 | tf_op jit(solution)/shard_map/while/body/eval_jaxpr/ppermute | solution.py:10
  414.2 2.8 gather_fusion
  416.9 5.2 bitcast_add_fusion.2
  422.4 16.8 %collective-permute-done = bf16[2,512,512]{2,1,0:T(8,128)(2,1)S(1)} collective-permute-done((bf16[2,512,512]{2,1,0:T(8,128)(2,1)S(1)}, bf16[2,512,512]{2,1,0:T(8,128)(2,1)S(1)}, u32[]{:S(2)}, u32[]{:S(2)}) %collective-permute-start) | collective-permute-done | bytes 1048608 | tf_op jit(solution)/shard_map/while/body/eval_jaxpr/ppermute | solution.py:10
  439.3 2.8 gather_fusion
  442.0 5.2 bitcast_add_fusion.2
  447.5 16.8 %collective-permute-done = bf16[2,512,512]{2,1,0:T(8,128)(2,1)S(1)} collective-permute-done((bf16[2,512,512]{2,1,0:T(8,128)(2,1)S(1)}, bf16[2,512,512]{2,1,0:T(8,128)(2,1)S(1)}, u32[]{:S(2)}, u32[]{:S(2)}) %collective-permute-start) | collective-permute-done | bytes 1048608 | tf_op jit(solution)/shard_map/while/body/eval_jaxpr/ppermute | solution.py:10
  464.4 2.8 gather_fusion
  467.1 5.2 bitcast_add_fusion.2
  472.5 2.0 maximum_convert_fusion
  479.8 18.2 %all-to-all-start = ((bf16[8,2,64,512]{3,2,1,0:T(8,128)(2,1)}), bf16[8,2,64,512]{3,2,1,0:T(8,128)(2,1)}, u32[]{:S(2)}, u32[]{:S(2)}) async-start(bf16[8,2,64,512]{3,2,1,0:T(8,128)(2,1)} %fusion.27), calls=%async_computation | async-start | bytes 2097152 | tf_op jit(solution)/shard_map/all_to_all | solution.py:68
  498.0 15.1 %all-to-all-done = bf16[8,2,64,512]{3,2,1,0:T(8,128)(2,1)} async-done(((bf16[8,2,64,512]{3,2,1,0:T(8,128)(2,1)}), bf16[8,2,64,512]{3,2,1,0:T(8,128)(2,1)}, u32[]{:S(2)}, u32[]{:S(2)}) %all-to-all-start) | async-done | bytes 1048608 | tf_op jit(solution)/shard_map/all_to_all | solution.py:68
  513.0 60.7 %while.30 = (s32[]{:T(128)}, f32[64,512]{1,0:T(8,128)S(1)}, bf16[16,64,512]{2,1,0:T(8,128)(2,1)}, bf16[16,64,512]{2,1,0:T(8,128)(2,1)}, bf16[512,1536]{1,0:T(8,1...) while((s32[]{:T(128)}, f32[64,512]{1,0:T(8,128)S(1)}, ...), condition=%wide.region_3.4_spmd, body=%wide.region_2.3_spmd.sunk | while | flops 201883648 | bytes 5246037 | solution.py:79
  514.3 1.8 fusion.63
  518.1 1.8 fusion.63
  521.9 1.8 fusion.63
  529.4 1.8 fusion.63
  533.2 1.8 fusion.63
  537.0 1.8 fusion.63
  552.2 1.8 fusion.63
  559.8 1.8 fusion.63
  573.7 19.4 %all_to_all.23 = bf16[16,64,512]{2,1,0:T(8,128)(2,1)S(1)} all-to-all(bf16[16,64,512]{2,1,0:T(8,128)(2,1)} %get-tuple-element.198), channel_id=1, replica_groups=mesh['tm'=8,'dom'=16] {'tm'}, dimensions={0} | all-to-all | bytes 2097152 | tf_op jit(solution)/shard_map/all_to_all | solution.py:80
  (126 shorter events, 60.4 us)
Async XLA Ops:
  0.0 498.0 %copy-start = (f32[512,512]{1,0:T(8,128)S(1)}, f32[512,512]{1,0:T(8,128)}, u32[]{:S(2)}) copy-start(f32[512,512]{1,0:T(8,128)} %param.17) | copy-start | bytes 3145732
  7.1 8.5 %copy-start.3 = (bf16[32,128,512]{2,1,0:T(8,128)(2,1)S(1)}, bf16[32,128,512]{2,1,0:T(8,128)(2,1)}, u32[]{:S(2)}) copy-start(bf16[32,128,512]{2,1,0:T(8,128)(2,1)} %gather_fusion.1) | copy-start | bytes 12582916
  15.6 6.4 %copy-start.2 = (bf16[2,4,16,4,128,128]{5,4,3,1,0,2:T(8,128)(2,1)}, bf16[2,4,16,4,128,128]{5,4,3,1,0,2:T(8,128)(2,1)S(1)}, u32[]{:S(2)}) copy-start(bf16[2,4,16,4,128,128]{5,4,3,1,0,2:T(8,128)(2,1)S(1)} %copy_multiply_fusion) | copy-start | bytes 50331652
  22.0 29.9 %collective-permute-start = (bf16[2,512,512]{2,1,0:T(8,128)(2,1)S(1)}, bf16[2,512,512]{2,1,0:T(8,128)(2,1)S(1)}, u32[]{:S(2)}, u32[]{:S(2)}) collective-permute-start(bf16[2,512,512]{2,1,0:T(8,128)(2,1)S(1)} %get-tuple-element.334), channel_id=1, source_target_pairs={{15,0},{0,1},{1,2},{2,3},{3,4},{4,5},{5,6},{6,7},{7,8},{8,9},{9,10... | collective-permute-start | bytes 3145736 | tf_op jit(solution)/shard_map/while/body/eval_jaxpr/ppermute | solution.py:10
  59.9 26.9 %collective-permute-start = (bf16[2,512,512]{2,1,0:T(8,128)(2,1)S(1)}, bf16[2,512,512]{2,1,0:T(8,128)(2,1)S(1)}, u32[]{:S(2)}, u32[]{:S(2)}) collective-permute-start(bf16[2,512,512]{2,1,0:T(8,128)(2,1)S(1)} %get-tuple-element.334), channel_id=1, source_target_pairs={{15,0},{0,1},{1,2},{2,3},{3,4},{4,5},{5,6},{6,7},{7,8},{8,9},{9,10... | collective-permute-start | bytes 3145736 | tf_op jit(solution)/shard_map/while/body/eval_jaxpr/ppermute | solution.py:10
  94.8 26.0 %collective-permute-start = (bf16[2,512,512]{2,1,0:T(8,128)(2,1)S(1)}, bf16[2,512,512]{2,1,0:T(8,128)(2,1)S(1)}, u32[]{:S(2)}, u32[]{:S(2)}) collective-permute-start(bf16[2,512,512]{2,1,0:T(8,128)(2,1)S(1)} %get-tuple-element.334), channel_id=1, source_target_pairs={{15,0},{0,1},{1,2},{2,3},{3,4},{4,5},{5,6},{6,7},{7,8},{8,9},{9,10... | collective-permute-start | bytes 3145736 | tf_op jit(solution)/shard_map/while/body/eval_jaxpr/ppermute | solution.py:10
  128.9 25.1 %collective-permute-start = (bf16[2,512,512]{2,1,0:T(8,128)(2,1)S(1)}, bf16[2,512,512]{2,1,0:T(8,128)(2,1)S(1)}, u32[]{:S(2)}, u32[]{:S(2)}) collective-permute-start(bf16[2,512,512]{2,1,0:T(8,128)(2,1)S(1)} %get-tuple-element.334), channel_id=1, source_target_pairs={{15,0},{0,1},{1,2},{2,3},{3,4},{4,5},{5,6},{6,7},{7,8},{8,9},{9,10... | collective-permute-start | bytes 3145736 | tf_op jit(solution)/shard_map/while/body/eval_jaxpr/ppermute | solution.py:10
  162.0 24.3 %collective-permute-start = (bf16[2,512,512]{2,1,0:T(8,128)(2,1)S(1)}, bf16[2,512,512]{2,1,0:T(8,128)(2,1)S(1)}, u32[]{:S(2)}, u32[]{:S(2)}) collective-permute-start(bf16[2,512,512]{2,1,0:T(8,128)(2,1)S(1)} %get-tuple-element.334), channel_id=1, source_target_pairs={{15,0},{0,1},{1,2},{2,3},{3,4},{4,5},{5,6},{6,7},{7,8},{8,9},{9,10... | collective-permute-start | bytes 3145736 | tf_op jit(solution)/shard_map/while/body/eval_jaxpr/ppermute | solution.py:10
  194.4 23.4 %collective-permute-start = (bf16[2,512,512]{2,1,0:T(8,128)(2,1)S(1)}, bf16[2,512,512]{2,1,0:T(8,128)(2,1)S(1)}, u32[]{:S(2)}, u32[]{:S(2)}) collective-permute-start(bf16[2,512,512]{2,1,0:T(8,128)(2,1)S(1)} %get-tuple-element.334), channel_id=1, source_target_pairs={{15,0},{0,1},{1,2},{2,3},{3,4},{4,5},{5,6},{6,7},{7,8},{8,9},{9,10... | collective-permute-start | bytes 3145736 | tf_op jit(solution)/shard_map/while/body/eval_jaxpr/ppermute | solution.py:10
  225.8 22.6 %collective-permute-start = (bf16[2,512,512]{2,1,0:T(8,128)(2,1)S(1)}, bf16[2,512,512]{2,1,0:T(8,128)(2,1)S(1)}, u32[]{:S(2)}, u32[]{:S(2)}) collective-permute-start(bf16[2,512,512]{2,1,0:T(8,128)(2,1)S(1)} %get-tuple-element.334), channel_id=1, source_target_pairs={{15,0},{0,1},{1,2},{2,3},{3,4},{4,5},{5,6},{6,7},{7,8},{8,9},{9,10... | collective-permute-start | bytes 3145736 | tf_op jit(solution)/shard_map/while/body/eval_jaxpr/ppermute | solution.py:10
  256.5 21.7 %collective-permute-start = (bf16[2,512,512]{2,1,0:T(8,128)(2,1)S(1)}, bf16[2,512,512]{2,1,0:T(8,128)(2,1)S(1)}, u32[]{:S(2)}, u32[]{:S(2)}) collective-permute-start(bf16[2,512,512]{2,1,0:T(8,128)(2,1)S(1)} %get-tuple-element.334), channel_id=1, source_target_pairs={{15,0},{0,1},{1,2},{2,3},{3,4},{4,5},{5,6},{6,7},{7,8},{8,9},{9,10... | collective-permute-start | bytes 3145736 | tf_op jit(solution)/shard_map/while/body/eval_jaxpr/ppermute | solution.py:10
  286.2 20.8 %collective-permute-start = (bf16[2,512,512]{2,1,0:T(8,128)(2,1)S(1)}, bf16[2,512,512]{2,1,0:T(8,128)(2,1)S(1)}, u32[]{:S(2)}, u32[]{:S(2)}) collective-permute-start(bf16[2,512,512]{2,1,0:T(8,128)(2,1)S(1)} %get-tuple-element.334), channel_id=1, source_target_pairs={{15,0},{0,1},{1,2},{2,3},{3,4},{4,5},{5,6},{6,7},{7,8},{8,9},{9,10... | collective-permute-start | bytes 3145736 | tf_op jit(solution)/shard_map/while/body/eval_jaxpr/ppermute | solution.py:10
  315.1 20.0 %collective-permute-start = (bf16[2,512,512]{2,1,0:T(8,128)(2,1)S(1)}, bf16[2,512,512]{2,1,0:T(8,128)(2,1)S(1)}, u32[]{:S(2)}, u32[]{:S(2)}) collective-permute-start(bf16[2,512,512]{2,1,0:T(8,128)(2,1)S(1)} %get-tuple-element.334), channel_id=1, source_target_pairs={{15,0},{0,1},{1,2},{2,3},{3,4},{4,5},{5,6},{6,7},{7,8},{8,9},{9,10... | collective-permute-start | bytes 3145736 | tf_op jit(solution)/shard_map/while/body/eval_jaxpr/ppermute | solution.py:10
  343.2 19.1 %collective-permute-start = (bf16[2,512,512]{2,1,0:T(8,128)(2,1)S(1)}, bf16[2,512,512]{2,1,0:T(8,128)(2,1)S(1)}, u32[]{:S(2)}, u32[]{:S(2)}) collective-permute-start(bf16[2,512,512]{2,1,0:T(8,128)(2,1)S(1)} %get-tuple-element.334), channel_id=1, source_target_pairs={{15,0},{0,1},{1,2},{2,3},{3,4},{4,5},{5,6},{6,7},{7,8},{8,9},{9,10... | collective-permute-start | bytes 3145736 | tf_op jit(solution)/shard_map/while/body/eval_jaxpr/ppermute | solution.py:10
  370.4 18.3 %collective-permute-start = (bf16[2,512,512]{2,1,0:T(8,128)(2,1)S(1)}, bf16[2,512,512]{2,1,0:T(8,128)(2,1)S(1)}, u32[]{:S(2)}, u32[]{:S(2)}) collective-permute-start(bf16[2,512,512]{2,1,0:T(8,128)(2,1)S(1)} %get-tuple-element.334), channel_id=1, source_target_pairs={{15,0},{0,1},{1,2},{2,3},{3,4},{4,5},{5,6},{6,7},{7,8},{8,9},{9,10... | collective-permute-start | bytes 3145736 | tf_op jit(solution)/shard_map/while/body/eval_jaxpr/ppermute | solution.py:10
  396.7 17.4 %collective-permute-start = (bf16[2,512,512]{2,1,0:T(8,128)(2,1)S(1)}, bf16[2,512,512]{2,1,0:T(8,128)(2,1)S(1)}, u32[]{:S(2)}, u32[]{:S(2)}) collective-permute-start(bf16[2,512,512]{2,1,0:T(8,128)(2,1)S(1)} %get-tuple-element.334), channel_id=1, source_target_pairs={{15,0},{0,1},{1,2},{2,3},{3,4},{4,5},{5,6},{6,7},{7,8},{8,9},{9,10... | collective-permute-start | bytes 3145736 | tf_op jit(solution)/shard_map/while/body/eval_jaxpr/ppermute | solution.py:10
  422.2 17.0 %collective-permute-start = (bf16[2,512,512]{2,1,0:T(8,128)(2,1)S(1)}, bf16[2,512,512]{2,1,0:T(8,128)(2,1)S(1)}, u32[]{:S(2)}, u32[]{:S(2)}) collective-permute-start(bf16[2,512,512]{2,1,0:T(8,128)(2,1)S(1)} %get-tuple-element.334), channel_id=1, source_target_pairs={{15,0},{0,1},{1,2},{2,3},{3,4},{4,5},{5,6},{6,7},{7,8},{8,9},{9,10... | collective-permute-start | bytes 3145736 | tf_op jit(solution)/shard_map/while/body/eval_jaxpr/ppermute | solution.py:10
  447.3 17.0 %collective-permute-start = (bf16[2,512,512]{2,1,0:T(8,128)(2,1)S(1)}, bf16[2,512,512]{2,1,0:T(8,128)(2,1)S(1)}, u32[]{:S(2)}, u32[]{:S(2)}) collective-permute-start(bf16[2,512,512]{2,1,0:T(8,128)(2,1)S(1)} %get-tuple-element.334), channel_id=1, source_target_pairs={{15,0},{0,1},{1,2},{2,3},{3,4},{4,5},{5,6},{6,7},{7,8},{8,9},{9,10... | collective-permute-start | bytes 3145736 | tf_op jit(solution)/shard_map/while/body/eval_jaxpr/ppermute | solution.py:10
  472.4 40.6 %copy-start.1 = (bf16[512,1536]{1,0:T(8,128)(2,1)S(1)}, bf16[512,1536]{1,0:T(8,128)(2,1)}, u32[]{:S(2)}) copy-start(bf16[512,1536]{1,0:T(8,128)(2,1)} %param.19) | copy-start | bytes 4718596
  472.4 40.6 %copy-start.4 = (f32[512]{0:T(512)S(1)}, f32[512]{0:T(512)}, u32[]{:S(2)}) copy-start(f32[512]{0:T(512)} %param.21) | copy-start | bytes 6148
  479.8 33.3 %all-to-all-start = ((bf16[8,2,64,512]{3,2,1,0:T(8,128)(2,1)}), bf16[8,2,64,512]{3,2,1,0:T(8,128)(2,1)}, u32[]{:S(2)}, u32[]{:S(2)}) async-start(bf16[8,2,64,512]{3,2,1,0:T(8,128)(2,1)} %fusion.27), calls=%async_computation | async-start | bytes 2097152 | tf_op jit(solution)/shard_map/all_to_all | solution.py:68
